TPU v7x, 256 devices: a whole 4x4x8 slice. The times are simulated.
256 devices in a mesh: rows: 64 (over y_lo, z, x), blk: 4 (over y_hi, core).
Axes of the slice: x: 4, y: 4 (y_hi: 2, y_lo: 2; y = y_hi * 2 + y_lo), z: 8, core: 2. Of those that a mesh axis runs over, the one named last changes fastest.
Arguments:
- block_weight: bfloat16 [64, 4, 4, 64, 128, 128], P('rows', 'blk'), may hold values from 0.049804688 to 50
- block_row: int32 [64, 4, 4, 64], P('rows', 'blk'), may hold values from 0 to 15, as said below
- block_col: int32 [64, 4, 4, 64], P('rows', 'blk'), may hold values from 0 to 7, as said below
- block_count: int32 [64, 4, 4], P('rows', 'blk'), may hold values from 1 to 64, as said below
- block_samples: int32 [64, 4, 4, 64], P('rows', 'blk'), may hold values from 1 to 8
- row_degree: float32 [64, 4, 2048], P('rows', 'blk'), may hold values from 0.125 to 8
- col_degree: float32 [4, 1024], P('blk', 'rows'), may hold values from 1 to 8
- test_matrix: bfloat16 [4, 1024, 128], P('blk', 'rows'), may hold values from -6 to 6
Outputs:
- basis: float32 [64, 4, 2048, 128], P('rows', 'blk')
- triangle: float32 [128, 128], replicated
Inputs may be any that keep to these rules, and one draw needn't show every extreme that they name: Within one band and slab, the slots k < 64 hold distinct (block_row, block_col) pairs. `block_col`: see block_row: pairs are distinct within one band and slab. `block_count`: some band and slab has all 64 slots live in every draw.
All inputs are finite; a program needn't handle non-finite values.
Results may differ from a plain program's by a relative error of at most 0.0065.
Values may be sent and summed in bfloat16 or wider, within the bound.
A program may use at most 64 MiB of HBM per device.

v0:
```python
import jax
import jax.numpy as jnp
from jax import lax
from jax.sharding import PartitionSpec as P

scale_factor = 16.0


def passed_along(block, axis, distance):
    devices = range(lax.axis_size(axis))
    route = [((i - distance) % len(devices), i) for i in devices]
    return lax.ppermute(block, axis, route)


def tile_update(
    running, weights, rows_idx, cols_idx, live_count, samples, row_deg, slab_rows, slab_deg
):
    block_edge = weights.shape[-1]
    capacity = weights.shape[0]
    band_blocks = running.shape[0]
    slab_blocks = slab_rows.shape[0] // block_edge
    slab_tiles = slab_rows.reshape(slab_blocks, block_edge, slab_rows.shape[1])
    picked = slab_tiles[cols_idx]
    col_d = slab_deg.reshape(slab_blocks, block_edge)[cols_idx]
    row_d = row_deg.reshape(band_blocks, block_edge)[rows_idx]
    scaled_ratio = (
        scale_factor
        * weights.astype(jnp.float32)
        / (samples.astype(jnp.float32)[:, None, None] * row_d[:, :, None] * col_d[:, None, :])
    )
    entries = jnp.log(jnp.maximum(scaled_ratio, 1.0)).astype(jnp.bfloat16)
    products = jnp.einsum("kij,kjc->kic", entries, picked, preferred_element_type=jnp.float32)
    alive_mask = (jnp.arange(capacity, dtype=jnp.int32) < live_count).astype(jnp.float32)
    chooser = (rows_idx[None, :] == jnp.arange(band_blocks, dtype=jnp.int32)[:, None]).astype(
        jnp.float32
    ) * alive_mask[None, :]
    return running + jnp.einsum("rk,kic->ric", chooser, products, precision=lax.Precision.HIGHEST)


def body(
    block_weight,
    block_row,
    block_col,
    block_count,
    block_samples,
    row_degree,
    col_degree,
    test_matrix,
):
    loop_size = lax.axis_size("blk")
    position = lax.axis_index("blk")
    weights_all = block_weight[0, 0]
    rows_all = block_row[0, 0]
    cols_all = block_col[0, 0]
    counts_all = block_count[0, 0]
    samples_all = block_samples[0, 0]
    row_deg = row_degree[0, 0]
    block_edge = weights_all.shape[-1]
    band_blocks = row_deg.shape[0] // block_edge
    running = jnp.zeros((band_blocks, block_edge, test_matrix.shape[2]), jnp.float32)
    piece_pair = (test_matrix, col_degree)
    for t in range(loop_size):
        if t > 0:
            piece_pair = (
                passed_along(piece_pair[0], "blk", 1),
                passed_along(piece_pair[1].astype(jnp.bfloat16), "blk", 1).astype(jnp.float32),
            )
        slab_rows, slab_deg = (
            lax.all_gather(piece_pair[0], "rows", axis=1, tiled=True),
            lax.all_gather(piece_pair[1].astype(jnp.bfloat16), "rows", axis=1, tiled=True).astype(
                jnp.float32
            ),
        )
        slab_index = (position - t) % loop_size
        apply_slab_rows = slab_rows[0]
        apply_slab_deg = slab_deg[0]
        slab_index = jnp.asarray(slab_index)
        running = tile_update(
            running,
            lax.dynamic_index_in_dim(weights_all, slab_index, 0, keepdims=False),
            lax.dynamic_index_in_dim(rows_all, slab_index, 0, keepdims=False),
            lax.dynamic_index_in_dim(cols_all, slab_index, 0, keepdims=False),
            lax.dynamic_index_in_dim(counts_all, slab_index, 0, keepdims=False),
            lax.dynamic_index_in_dim(samples_all, slab_index, 0, keepdims=False),
            row_deg,
            apply_slab_rows,
            apply_slab_deg,
        )
    flat_rows = running.reshape(band_blocks * block_edge, running.shape[2])
    gram_local = jnp.dot(
        flat_rows.T, flat_rows, precision=lax.Precision.HIGHEST, preferred_element_type=jnp.float32
    )
    gram_total = lax.psum(gram_local, ("rows", "blk"))
    lower_factor = jnp.linalg.cholesky(gram_total)
    total_rows = flat_rows.shape[0] * lax.axis_size("rows") * loop_size
    root = jnp.sqrt(jnp.float32(total_rows))
    basis_rows = (
        lax.linalg.triangular_solve(
            lower_factor, flat_rows, left_side=False, lower=True, transpose_a=True
        )
        * root
    )
    return (basis_rows.reshape(1, 1, flat_rows.shape[0], flat_rows.shape[1]), lower_factor.T / root)


def solution(mesh):
    placed = (
        P("rows", "blk", None, None, None, None),
        P("rows", "blk", None, None),
        P("rows", "blk", None, None),
        P("rows", "blk", None),
        P("rows", "blk", None, None),
        P("rows", "blk", None),
        P("blk", "rows"),
        P("blk", "rows", None),
    )
    return jax.shard_map(
        body,
        mesh=mesh,
        in_specs=placed,
        out_specs=(P("rows", "blk", None, None), P()),
        check_vma=False,
    )
```

profile of v0, /device:TPU:1, one launch (start us, length us, event | category | flops | bytes accessed | tf_op | source)
XLA Modules:
  0.0 1118.6 jit_solution(2050559915229179514)
XLA Ops:
  7.2 0.0 all-reduce.7.cloned.1.call-start
  7.2 4.4 collective-permute-start.1
  11.6 0.7 convert_bitcast_fusion
  12.3 0.0 collective-permute-start
  12.3 132.2 %all_gather.25 = bf16[1,1024,128]{2,1,0:T(8,128)(2,1)S(1)} all-gather(bf16[1,16,128]{2,1,0:T(8,128)(2,1)} %param.15), channel_id=1, replica_groups=mesh['rows'=64,'blk'=4] {'rows'}, dimensions={1}, use_global_device_ids=true | all-gather | bytes 266240 | tf_op jit(solution)/shard_map/all_gather | solution.py:69
  144.4 1.4 fusion.107
  145.9 0.8 fusion.90
  146.7 0.8 fusion.102
  147.6 1.4 constant_dynamic-slice_fusion.2
  149.0 0.6 compare_convert_fusion.2
  149.7 0.6 gather_fusion.3
  150.3 0.6 gather_fusion
  150.9 0.6 compare_convert_fusion.3
  151.6 0.6 gather_fusion.6
  152.2 1.1 compare_convert_fusion.1
  153.3 0.6 gather_fusion.9
  153.8 1.1 compare_convert_fusion
  155.0 1.3 dynamic-slice.20
  156.9 0.1 broadcast_multiply_fusion.2
  157.0 1.0 gather_fusion.2
  157.9 0.1 broadcast_multiply_fusion.3
  158.0 0.1 broadcast_multiply_fusion.1
  158.1 0.1 broadcast_multiply_fusion
  158.2 0.2 dynamic-update-slice.3
  158.4 0.2 dynamic-update-slice.4
  158.6 29.4 %collective-permute-start.2 = (bf16[1,16]{1,0:T(2,128)(2,1)S(1)}, bf16[1,16]{1,0:T(2,128)(2,1)S(1)}, u32[]{:S(2)}, u32[]{:S(2)}) collective-permute-start(bf16[1,16]{1,0:T(2,128)(2,1)S(1)} %collective-permute-done), channel_id=1, source_target_pairs={{3,0},{0,1},{1,2},{2,3},{7,4},{4,5},{5,6},{6,7},{11,8},{8,9},{9,10... | collective-permute-start | bytes 104 | tf_op jit(solution)/shard_map/ppermute | solution.py:12
  188.0 0.7 collective-permute-done.2
  188.7 0.2 dynamic-update-slice.5
  188.9 3.8 collective-permute-start.4
  192.7 0.7 collective-permute-done.4
  193.5 0.2 dynamic-update-slice.6
  193.6 127.1 %all-reduce.4 = (bf16[1024]{0:T(1024)(128)(2,1)S(1)}, bf16[1024]{0:T(1024)(128)(2,1)S(1)}, bf16[1024]{0:T(1024)(128)(2,1)S(1)}, bf16[1024]{0:T(1024)(128)(2,1)S(1)}) all-reduce(bf16[1024]{0:T(1024)(128)(2,1)S(1)} %dynamic-update-slice.4, bf16[1024]{0:T(1024)(128)(2,1)S(1)} %dynamic-update-slice.3, ...), channel_id=1, replica_groups=mesh['rows'=64,'blk'=4] {'rows'}, use_global_device_ids=true, to_apply=%add.1 | all-reduce | flops 4096 | bytes 16384
  320.8 0.6 gather_fusion.1
  321.4 4.1 fusion.21
  325.5 0.6 gather_fusion.4
  326.1 0.6 gather_fusion.7
  326.7 0.6 gather_fusion.10
  327.3 124.8 %all_gather.27 = bf16[1,1024,128]{2,1,0:T(8,128)(2,1)S(1)} all-gather(bf16[1,16,128]{2,1,0:T(8,128)(2,1)S(1)} %collective-permute-done.1), channel_id=1, replica_groups=mesh['rows'=64,'blk'=4] {'rows'}, dimensions={1}, use_global_device_ids=true | all-gather | bytes 266240 | tf_op jit(solution)/shard_map/all_gather | solution.py:69
  452.1 0.9 gather_fusion.5
  453.1 3.6 fusion.23
  456.7 4.4 fusion.16
  461.0 60.1 %collective-permute-start.3 = (bf16[1,16,128]{2,1,0:T(8,128)(2,1)S(1)}, bf16[1,16,128]{2,1,0:T(8,128)(2,1)S(1)}, u32[]{:S(2)}, u32[]{:S(2)}) collective-permute-start(bf16[1,16,128]{2,1,0:T(8,128)(2,1)S(1)} %collective-permute-done.1), channel_id=1, source_target_pairs={{3,0},{0,1},{1,2},{2,3},{7,4},{4,5},{5,6},{6,7},{11,8},{8,9},{9,10... | collective-permute-start | bytes 12296 | tf_op jit(solution)/shard_map/ppermute | solution.py:12
  521.1 4.4 fusion.49
  525.5 124.0 %all_gather.29 = bf16[1,1024,128]{2,1,0:T(8,128)(2,1)S(1)} all-gather(bf16[1,16,128]{2,1,0:T(8,128)(2,1)S(1)} %collective-permute-done.3), channel_id=1, replica_groups=mesh['rows'=64,'blk'=4] {'rows'}, dimensions={1}, use_global_device_ids=true | all-gather | bytes 266240 | tf_op jit(solution)/shard_map/all_gather | solution.py:69
  649.6 1.0 gather_fusion.8
  650.6 3.6 fusion.25
  654.2 27.5 %collective-permute-start.5 = (bf16[1,16,128]{2,1,0:T(8,128)(2,1)S(1)}, bf16[1,16,128]{2,1,0:T(8,128)(2,1)S(1)}, u32[]{:S(2)}, u32[]{:S(2)}) collective-permute-start(bf16[1,16,128]{2,1,0:T(8,128)(2,1)S(1)} %copy-done.3), channel_id=1, source_target_pairs={{3,0},{0,1},{1,2},{2,3},{7,4},{4,5},{5,6},{6,7},{11,8},{8,9},{9,10... | collective-permute-start | bytes 12296 | tf_op jit(solution)/shard_map/ppermute | solution.py:12
  681.8 4.4 fusion.52
  686.2 125.7 %all_gather.31 = bf16[1,1024,128]{2,1,0:T(8,128)(2,1)S(1)} all-gather(bf16[1,16,128]{2,1,0:T(8,128)(2,1)S(1)} %collective-permute-done.5), channel_id=1, replica_groups=mesh['rows'=64,'blk'=4] {'rows'}, dimensions={1}, use_global_device_ids=true | all-gather | bytes 266240 | tf_op jit(solution)/shard_map/all_gather | solution.py:69
  811.9 2.1 gather_fusion.11
  814.0 3.3 fusion.27
  817.4 4.4 fusion.55
  821.8 2.5 convolution_bitcast_fusion
  824.3 0.0 all-reduce.7.cloned.1.call-update
  824.4 0.3 copy.15
  824.7 259.5 %all-reduce.7.cloned.1.call-done = f32[128,128]{0,1:T(8,128)} async-done(((f32[128,128]{0,1:T(8,128)}), f32[128,128]{0,1:T(8,128)}) %all-reduce.7.cloned.1.call-update) | async-done | bytes 65552 | tf_op jit(solution)/shard_map/psum | solution.py:93
  1084.2 0.9 copy.19
  1085.1 0.9 fusion.59
  1086.0 11.7 %cholesky.16 = f32[128,128]{1,0:T(8,128)S(1)} custom-call(f32[128,128]{1,0:T(8,128)S(1)} %fusion.59), custom_call_target="Cholesky" | custom-call | tf_op jit(solution)/shard_map/jit(cholesky)/cholesky | solution.py:94
  1097.7 0.6 compare_reduce_fusion
  1098.4 0.7 multiply_bitcast_fusion
  1099.0 9.8 custom-call.6
  1108.9 0.7 copy.20
  1109.6 1.9 fusion.20
  (37 shorter events, 0.2 us)
Async XLA Ops:
  7.2 142.5 %copy-start = (f32[1,1,2048]{2,1,0:T(1,128)S(1)}, f32[1,1,2048]{2,1,0:T(1,128)}, u32[]{:S(2)}) copy-start(f32[1,1,2048]{2,1,0:T(1,128)} %param.13) | copy-start | bytes 24580
  7.2 1077.0 %all-reduce.7.cloned.1.call-start = ((), (), s32[]{:S(2)}) async-start(), calls=%async_computation | async-start | bytes 131072 | tf_op jit(solution)/shard_map/psum | solution.py:93
  7.2 320.1 %collective-permute-start.1 = (bf16[1,16,128]{2,1,0:T(8,128)(2,1)}, bf16[1,16,128]{2,1,0:T(8,128)(2,1)S(1)}, u32[]{:S(2)}, u32[]{:S(2)}) collective-permute-start(bf16[1,16,128]{2,1,0:T(8,128)(2,1)} %param.15), channel_id=1, source_target_pairs={{3,0},{0,1},{1,2},{2,3},{7,4},{4,5},{5,6},{6,7},{11,8},{8,9},{9,10... | collective-permute-start | bytes 12296 | tf_op jit(solution)/shard_map/ppermute | solution.py:12
  12.3 146.1 %collective-permute-start = (bf16[1,16]{1,0:T(2,128)(2,1)S(1)}, bf16[1,16]{1,0:T(2,128)(2,1)S(1)}, u32[]{:S(2)}, u32[]{:S(2)}) collective-permute-start(bf16[1,16]{1,0:T(2,128)(2,1)S(1)} %get-tuple-element.33), channel_id=1, source_target_pairs={{3,0},{0,1},{1,2},{2,3},{7,4},{4,5},{5,6},{6,7},{11,8},{8,9},{9,10... | collective-permute-start | bytes 104 | tf_op jit(solution)/shard_map/ppermute | solution.py:12
  158.6 30.1 %collective-permute-start.2 = (bf16[1,16]{1,0:T(2,128)(2,1)S(1)}, bf16[1,16]{1,0:T(2,128)(2,1)S(1)}, u32[]{:S(2)}, u32[]{:S(2)}) collective-permute-start(bf16[1,16]{1,0:T(2,128)(2,1)S(1)} %collective-permute-done), channel_id=1, source_target_pairs={{3,0},{0,1},{1,2},{2,3},{7,4},{4,5},{5,6},{6,7},{11,8},{8,9},{9,10... | collective-permute-start | bytes 104 | tf_op jit(solution)/shard_map/ppermute | solution.py:12
  188.9 4.5 collective-permute-start.4
  456.7 64.4 %copy-start.1 = (f32[64,128,128]{2,1,0:T(8,128)S(1)}, f32[64,128,128]{2,1,0:T(8,128)}, u32[]{:S(2)}) copy-start(f32[64,128,128]{2,1,0:T(8,128)} %fusion.21) | copy-start | bytes 12582916
  461.0 64.5 %collective-permute-start.3 = (bf16[1,16,128]{2,1,0:T(8,128)(2,1)S(1)}, bf16[1,16,128]{2,1,0:T(8,128)(2,1)S(1)}, u32[]{:S(2)}, u32[]{:S(2)}) collective-permute-start(bf16[1,16,128]{2,1,0:T(8,128)(2,1)S(1)} %collective-permute-done.1), channel_id=1, source_target_pairs={{3,0},{0,1},{1,2},{2,3},{7,4},{4,5},{5,6},{6,7},{11,8},{8,9},{9,10... | collective-permute-start | bytes 12296 | tf_op jit(solution)/shard_map/ppermute | solution.py:12
  525.5 124.1 %copy-start.2 = (bf16[1,16,128]{2,1,0:T(8,128)(2,1)}, bf16[1,16,128]{2,1,0:T(8,128)(2,1)S(1)}, u32[]{:S(2)}) copy-start(bf16[1,16,128]{2,1,0:T(8,128)(2,1)S(1)} %collective-permute-done.3) | copy-start | bytes 12292
  650.5 3.7 copy-start.3
  650.5 31.2 %copy-start.5 = (s32[64]{0:T(128)S(1)}, s32[64]{0:T(128)}, u32[]{:S(2)}) copy-start(s32[64]{0:T(128)} %get-tuple-element.15) | copy-start | bytes 772
  650.5 31.2 %copy-start.7 = (f32[64]{0:T(128)S(1)}, f32[64]{0:T(128)}, u32[]{:S(2)}) copy-start(f32[64]{0:T(128)} %compare_convert_fusion.1) | copy-start | bytes 772
  654.2 32.0 %collective-permute-start.5 = (bf16[1,16,128]{2,1,0:T(8,128)(2,1)S(1)}, bf16[1,16,128]{2,1,0:T(8,128)(2,1)S(1)}, u32[]{:S(2)}, u32[]{:S(2)}) collective-permute-start(bf16[1,16,128]{2,1,0:T(8,128)(2,1)S(1)} %copy-done.3), channel_id=1, source_target_pairs={{3,0},{0,1},{1,2},{2,3},{7,4},{4,5},{5,6},{6,7},{11,8},{8,9},{9,10... | collective-permute-start | bytes 12296 | tf_op jit(solution)/shard_map/ppermute | solution.py:12
  814.0 3.4 copy-start.4
  814.0 3.4 copy-start.6
Sparse Core Ops, SparseCore 0:
  824.5 259.6 all-reduce.6
where the time goes:
time: 1120 us
  blocking collectives  634 us (57%)
  waiting for transfers between devices  261 us (23%)
  starting transfers between devices  125 us (11%)
  matrix products  36.7 us (3%)
  other arithmetic  29.9 us (3%)
  local copies, waits for them, and re-layouts  16.8 us (2%)
  between operations  15.2 us (1%)
    all_gather x4, blocking collectives, body(): lax.all_gather(piece_pair[0], 'rows', axis=1, tiled=True)  507 us
    psum x1, waiting for transfers between devices, body(): gram_total = lax.psum(gram_local, ('rows', 'blk'))  259 us
    unnamed x1, blocking collectives  127 us
    ppermute x6, starting transfers between devices, passed_along(): return lax.ppermute(block, axis, route)  125 us
  transfers between devices with their start and end apart: 7, of which 3 were waited for; matrix products, arithmetic and copies ran while one was open for 3% of the time, Pallas kernels for 0%

commit v1 on v0

v1 whole, which is shorter than its diff:
```python
import functools, jax, jax.numpy as jnp, numpy as np
from jax.sharding import PartitionSpec as P
from jax import lax
from jax.experimental import pallas as pl
from jax.experimental.pallas import tpu as pltpu
F32=jnp.float32; BF16=jnp.bfloat16

def split(x):
    hi = x.astype(BF16)
    return hi, (x - hi.astype(F32)).astype(BF16)

def entries_kernel(row_s, col_s, smp_s, cnt_s, row_v, col_v, cnt_v, w_hbm, rd_ref, cdp_ref, t_ref, s_ref, g_ref, wbuf, ebuf, rinv, cinv, posv, poss, sem, psem):
    copies = [pltpu.make_async_copy(w_hbm.at[pl.ds(i*32,32)], wbuf.at[pl.ds(i*32,32)], sem.at[i]) for i in range(8)]
    for c in copies: c.start()
    kk = lax.broadcasted_iota(jnp.int32, (1,64),1)
    for s in range(4):
        rc = row_v[s:s+1,:]*8 + col_v[s:s+1,:]
        rc = jnp.where(kk < cnt_s[s], rc, -1)
        m = (lax.broadcasted_iota(jnp.int32,(128,64),0) == rc)
        m = jnp.where(m, 1.0, 0.0).astype(BF16)
        kv = jnp.broadcast_to((kk-64), (8,64)).astype(F32).astype(BF16)
        p = lax.dot_general(kv, m, (((1,),(1,)),((),())), preferred_element_type=F32)[0:1]
        p = p.astype(jnp.int32)
        posv[s:s+1,:] = jnp.where(p < 0, p + (64*s+64), 256)
    cp = pltpu.make_async_copy(posv, poss, psem); cp.start()
    r16 = 16.0 / rd_ref[...]
    for q in range(16):
        rinv[q] = jnp.broadcast_to(r16[q:q+1,:], (128,128)).T
    for bc in range(32):
        acc = cdp_ref[bc,0]
        for i in range(1,8): acc = acc + cdp_ref[bc,i]
        cinv[bc] = jnp.broadcast_to(1.0/acc, (8,128))
    ebuf[256] = jnp.zeros((128,128), BF16)
    for s in range(4):
        copies[2*s].wait(); copies[2*s+1].wait()
        def slot(k, _):
            q = row_s[s,k-64*s]; c = col_s[s,k-64*s]
            sm = 1.0 / jnp.full((8,128), smp_s[s,k-64*s], jnp.int32).astype(F32)
            b = cinv[s*8 + c] * sm
            a = rinv[q].reshape(16,8,128)
            w = wbuf[k].astype(F32).reshape(16,8,128)
            e = jnp.log(jnp.maximum(w*a*b[None], 1.0))
            ebuf[k] = e.reshape(128,128).astype(BF16)
            return 0
        lax.fori_loop(64*s, 64*s+64, slot, 0, unroll=2)
    cp.wait()
    def qpair(i, g):
        acc = jnp.zeros((256,128), F32)
        for s in range(4):
            for cp_ in range(4):
                blk=[]
                for dq in range(2):
                    q = 2*i+dq
                    blk.append(jnp.concatenate([ebuf[poss[s, q*8+2*cp_]], ebuf[poss[s, q*8+2*cp_+1]]],axis=1))
                lhs = jnp.concatenate(blk,axis=0)
                acc = acc + jnp.dot(lhs, t_ref[pl.ds((s*4+cp_)*256,256),:], preferred_element_type=F32)
        s_ref[pl.ds(i*256,256),:] = acc
        hi, lo = split(acc)
        return g + lax.dot_general(hi, jnp.concatenate([hi,lo],axis=1), (((0,),(0,)),((),())), preferred_element_type=F32)
    g = lax.fori_loop(0, 8, qpair, jnp.zeros((128,256),F32))
    g_ref[...] = g[:,:128] + g[:,128:] + g[:,128:].T

VM=pl.BlockSpec(memory_space=pltpu.VMEM); SM=pl.BlockSpec(memory_space=pltpu.SMEM); AN=pl.BlockSpec(memory_space=pl.ANY)
def entries(row, col, smp, cnt, w, rd, cdp, t):
    return pl.pallas_call(entries_kernel,
        out_shape=(jax.ShapeDtypeStruct((2048,128),F32), jax.ShapeDtypeStruct((128,128),F32)),
        in_specs=[SM,SM,SM,SM,VM,VM,VM,AN,VM,VM,VM], out_specs=(VM,VM),
        scratch_shapes=[pltpu.VMEM((256,128,128),BF16), pltpu.VMEM((257,128,128),BF16), pltpu.VMEM((16,128,128),F32), pltpu.VMEM((32,8,128),F32),
            pltpu.VMEM((4,128),jnp.int32), pltpu.SMEM((4,128),jnp.int32), pltpu.SemaphoreType.DMA((8,)), pltpu.SemaphoreType.DMA],
        name='entries')(row, col, smp, cnt, row, col, cnt.reshape(1,4), w.reshape(256,128,128), rd.reshape(16,128), cdp, t)

def eliminate(v, n=128):
    sub = lax.broadcasted_iota(jnp.int32,(8,128),0); lane = lax.broadcasted_iota(jnp.int32,(8,128),1)
    for p in range(16):
        P = v[8*p:8*p+8,:]
        for r in range(8):
            j = 8*p+r
            c = jnp.broadcast_to(P[:, j:j+1], (8,128))
            inv = lax.rsqrt(jnp.broadcast_to(c[r:r+1,:],(8,128)))
            row = jnp.where(lane==j, 1.0, jnp.broadcast_to(P[r:r+1,:],(8,128)))*inv
            m = jnp.where(sub>r, c*inv, 0.0)
            P = jnp.where(sub==r, row, jnp.where((lane==j)&(sub>r), 0.0, P) - m*row)
        v[8*p:8*p+8,:] = P
        if p<15:
            lo = 8*p+8
            rhs = jnp.where((lane < lo) & (lane - 8*p > sub), 0.0, P)
            d = lax.dot_general(P, rhs, (((0,),(0,)),((),())), precision=lax.Precision.HIGHEST, preferred_element_type=F32)
            old = v[lo:,:]
            lane2 = lax.broadcasted_iota(jnp.int32, old.shape, 1)
            old = jnp.where((lane2>=8*p)&(lane2<lo), 0.0, old)
            v[lo:,:] = old - d[lo:,:]

def finish_kernel(g_ref, s_ref, b_ref, tri_ref, v):
    v[...] = g_ref[...]
    eliminate(v)
    V = v[...]
    i = lax.broadcasted_iota(jnp.int32,(128,128),0); j = lax.broadcasted_iota(jnp.int32,(128,128),1)
    root = float(np.sqrt(np.float32(524288.0)))
    tri_ref[...] = jnp.where(j>i, V, jnp.where(j==i, 1.0/V, 0.0))*(1.0/root)
    X = jnp.where(j<=i, V, 0.0)*root
    xh, xl = split(X)
    xx = jnp.concatenate([xh,xl],axis=0)
    def step(n,_):
        sh, sl = split(s_ref[pl.ds(n*256,256),:])
        d = lax.dot_general(sh, xx, (((1,),(1,)),((),())), preferred_element_type=F32)
        e = lax.dot_general(sl, xh, (((1,),(1,)),((),())), preferred_element_type=F32)
        b_ref[pl.ds(n*256,256),:] = d[:,:128]+d[:,128:]+e
        return 0
    lax.fori_loop(0,8,step,0)

def finish(g, s):
    return pl.pallas_call(finish_kernel, out_shape=(jax.ShapeDtypeStruct((2048,128),F32), jax.ShapeDtypeStruct((128,128),F32)),
        in_specs=[VM,VM], out_specs=(VM,VM), scratch_shapes=[pltpu.VMEM((128,128),F32)],name='finish')(g,s)
MESH = pl.DeviceIdType.MESH

def place():
    r = lax.axis_index("rows"); b = lax.axis_index("blk")
    return b // 2, lax.rem(b, 2), r // 32, lax.rem(r // 4, 8), lax.rem(r, 4)

def device(y, core, z, x):
    return (lax.rem(y, 2) * 32 + z * 4 + x, (y // 2) * 2 + core)

def greet(peers):
    barrier = pltpu.get_barrier_semaphore()
    for p in peers:
        pl.semaphore_signal(barrier, inc=1, device_id=p, device_id_type=MESH)
    pl.semaphore_wait(barrier, len(peers))

def send(src, dst, ss, rs, dev):
    c = pltpu.make_async_remote_copy(src_ref=src, dst_ref=dst, send_sem=ss, recv_sem=rs, device_id=dev, device_id_type=MESH)
    c.start()
    return c

def axis_peers():
    yh, core, yl, z, x = place()
    y = yh * 2 + yl
    zs = [device(y, core, lax.rem(z + d, 8), x) for d in range(1, 8)]
    ys = [device(lax.rem(y + d, 4), core, z, x) for d in range(1, 4)]
    xs = [device(y, core, z, lax.rem(x + d, 4)) for d in range(1, 4)]
    return zs, ys, xs, device(y, 1 - core, z, x)

def gather_kernel(t_in, cd_in, t_out, cd_out, tb, cb, zs_s, zs_r, b_s, b_r, c_s, c_r, d_s, d_r, l_sem):
    yh, core, yl, z, x = place()
    zp, yp, xp, partner = axis_peers()
    tb[yh, core, yl, z, x] = t_in[...]
    lane = lax.broadcasted_iota(jnp.int32, (1, 128), 1)
    r8 = lax.rem(z, 2) * 4 + x
    cdl = jnp.where(lane // 16 == r8, jnp.concatenate([cd_in[...]] * 8, axis=1), 0.0)
    cb[yh, core, yl, z, x] = cdl
    greet(zp + yp + xp + [partner])
    def both(at, sems_s, sems_r, i, dev):
        return [send(tb.at[at], tb.at[at], sems_s.at[i, 0], sems_r.at[i, 0], dev),
                send(cb.at[at], cb.at[at], sems_s.at[i, 1], sems_r.at[i, 1], dev)]
    A = slice(None)
    cs = []
    for i, p in enumerate(zp):
        cs += both((yh, core, yl, z, x), zs_s, zs_r, i, p)
    for c in cs: c.wait()
    cs = []
    for i in range(3):
        cs += both((yh, core, yl, pl.ds(0, 4), x), b_s, b_r, 2 * i, yp[i])
        cs += both((yh, core, yl, pl.ds(4, 4), A), b_s, b_r, 2 * i + 1, xp[i]) if False else both((yh, core, yl, pl.ds(4, 4), x), b_s, b_r, 2 * i + 1, xp[i])
    for c in cs: c.wait()
    cs = []
    for i in range(3):
        for h in range(2):
            for l in range(2):
                cs += both((h, core, l, pl.ds(0, 4), x), c_s, c_r, 5 * i + 2 * h + l, xp[i])
        cs += both((yh, core, yl, pl.ds(4, 4)), c_s, c_r, 5 * i + 4, yp[i])
    for c in cs: c.wait()
    cs = []
    for h in range(2):
        cs += both((h, core), d_s, d_r, h, partner)
    for c in cs: c.wait()
    o = [pltpu.make_async_copy(tb, t_out, l_sem.at[0]), pltpu.make_async_copy(cb, cd_out, l_sem.at[1])]
    for c in o: c.start()
    for c in o: c.wait()

def gather(t, cd):
    dma = lambda *s: pltpu.SemaphoreType.DMA(s)
    tshape = (2, 2, 2, 8, 4, 16, 128); cshape = (2, 2, 2, 8, 4, 1, 128)
    return pl.pallas_call(gather_kernel, out_shape=(jax.ShapeDtypeStruct(tshape, BF16), jax.ShapeDtypeStruct(cshape, F32)),
        in_specs=[VM, VM], out_specs=(AN, AN),
        scratch_shapes=[pltpu.VMEM(tshape, BF16), pltpu.VMEM(cshape, F32), dma(7,2), dma(7,2), dma(6,2), dma(6,2), dma(15,2), dma(15,2), dma(2,2), dma(2,2), dma(2)],
        compiler_params=pltpu.CompilerParams(collective_id=0, has_side_effects=True), name="gather")(t, cd)

def reduce_phases(g, part, r1, r2, r3, res, s1s, s1r, s2s, s2r, s3s, s3r, s4s, s4r):
    yh, core, yl, z, x = place()
    y = yh * 2 + yl
    own = [x, y]
    def peer(half, d, c):
        return device(y, c, z, lax.rem(x + d, 4)) if half == 0 else device(lax.rem(y + d, 4), c, z, x)
    cs = []
    for half in range(2):
        for d in range(4):
            for dc in range(2):
                if d == 0 and dc == 0: continue
                c2 = lax.rem(core + dc, 2)
                o = lax.rem(own[half] + d, 4)
                cs.append(send(g.at[8 * c2 + 4 * half + o], r1.at[half, 2 * own[half] + core], s1s.at[half, 2 * d + dc], s1r.at[half, 2 * d + dc], peer(half, d, c2)))
        r1[half, 2 * own[half] + core] = g[8 * core + 4 * half + own[half]]
    for c in cs: c.wait()
    cs = []
    for half in range(2):
        a = r1[half, 0]
        for i in range(1, 8): a = a + r1[half, i]
        other = own[1 - half]
        r2[half, other] = a
        for d in range(1, 4):
            cs.append(send(r2.at[half, other], r2.at[half, other], s2s.at[half, d - 1], s2r.at[half, d - 1], peer(1 - half, d, core)))
    for c in cs: c.wait()
    for half in range(2):
        r3[z, half] = (r2[half, 0] + r2[half, 1]) + (r2[half, 2] + r2[half, 3])
    cs = []
    for d in range(1, 8):
        cs.append(send(r3.at[z], r3.at[z], s3s.at[d - 1], s3r.at[d - 1], device(y, core, lax.rem(z + d, 8), x)))
    for c in cs: c.wait()
    cs = []
    for half in range(2):
        a = ((r3[0, half] + r3[1, half]) + (r3[2, half] + r3[3, half])) + ((r3[4, half] + r3[5, half]) + (r3[6, half] + r3[7, half]))
        at = 8 * core + 4 * half + own[half]
        res[at] = a
        for d in range(4):
            for dc in range(2):
                if d == 0 and dc == 0: continue
                cs.append(send(res.at[at], res.at[at], s4s.at[half, 2 * d + dc], s4r.at[half, 2 * d + dc], peer(half, d, lax.rem(core + dc, 2))))
    for c in cs: c.wait()

def reduce_kernel(g, out, part, r1, r2, r3, res, *sems):
    yh, core, yl, z, x = place()
    y = yh * 2 + yl
    zp, yp, xp, partner = axis_peers()
    other = [device(lax.rem(y + d, 4), 1 - core, z, x) for d in range(1, 4)] + [device(y, 1 - core, z, lax.rem(x + d, 4)) for d in range(1, 4)]
    greet(zp + yp + xp + [partner] + other)
    reduce_phases(g, part, r1, r2, r3, res, *sems)
    out[...] = res[...]

def reduce_scratch():
    dma = lambda *s: pltpu.SemaphoreType.DMA(s)
    return [pltpu.VMEM((2,8,128),F32), pltpu.VMEM((2,8,8,128),F32), pltpu.VMEM((2,4,8,128),F32), pltpu.VMEM((8,2,8,128),F32), pltpu.VMEM((16,8,128),F32),
            dma(2,8),dma(2,8),dma(2,3),dma(2,3),dma(7),dma(7),dma(2,8),dma(2,8)]

def reduce_gram(g):
    return pl.pallas_call(reduce_kernel, out_shape=jax.ShapeDtypeStruct((16,8,128),F32), in_specs=[VM], out_specs=VM,
        scratch_shapes=reduce_scratch(), compiler_params=pltpu.CompilerParams(collective_id=1, has_side_effects=True), name="reduce")(g.reshape(16,8,128)).reshape(128,128)

def body(w, row, col, cnt, smp, rd, cd, t):
    tt, cc = gather(t[0], cd)
    s, g = entries(row[0,0], col[0,0], smp[0,0], cnt[0,0], w[0,0], rd[0,0], cc.reshape(32,8,1,128), tt.reshape(4096,128))
    g = reduce_gram(g)
    b, tri = finish(g, s)
    return b.reshape(1,1,2048,128), tri

def solution(mesh):
    placed = (P("rows","blk",None,None,None,None), P("rows","blk",None,None), P("rows","blk",None,None), P("rows","blk",None), P("rows","blk",None,None), P("rows","blk",None), P("blk","rows"), P("blk","rows",None))
    return jax.shard_map(body, mesh=mesh, in_specs=placed, out_specs=(P("rows","blk",None,None), P()), check_vma=False)
```

time: 1120 us -> 88.6 us (0.08)
  blocking collectives: 634 us -> 0 us
  waiting for transfers between devices: 261 us -> 0 us
  starting transfers between devices: 125 us -> 0 us
  Pallas kernels: 0 us -> 87.7 us
  matrix products: 36.7 us -> 0 us
  other arithmetic: 29.9 us -> 0 us
  local copies, waits for them, and re-layouts: 16.8 us -> 0 us
  between operations: 15.2 us -> 0.65 us
    all_gather x4 -> x0, blocking collectives: 507 us -> none  [body(): lax.all_gather(piece_pair[0], 'rows', axis=1, tiled=True)]
    psum x1 -> x0, waiting for transfers between devices: 259 us -> none  [body(): gram_total = lax.psum(gram_local, ('rows', 'blk'))]
    unnamed x1 -> x0, blocking collectives: 127 us -> none
    ppermute x6 -> x0, starting transfers between devices: 125 us -> none  [passed_along(): return lax.ppermute(block, axis, route)]
    pallas_call x0 -> x4, Pallas kernels: none -> 87.7 us  [the longest x1 28.4 us: gather(): pl.pallas_call(gather_kernel, out_shape=(jax.ShapeDtypeStruct(tshape, BF1...]
    dot_general x9 -> x0, matrix products: 34.8 us -> none  [the longest x4 17.6 us: tile_update(): jnp.einsum('rk,kic->ric', chooser, products, precision=lax.Precision.HIGH...]
    another operation x8 -> x0, other arithmetic: 22.2 us -> none  [the longest x3 12.4 us: body(): lower_factor = jnp.linalg.cholesky(gram_total)]
  transfers between devices with their start and end apart: 7 -> 0, of which waited for: 3 -> 0; matrix products, arithmetic and copies ran while one was open for 3% -> 0% of each run, Pallas kernels for 0% -> 0%
where the time goes in v1:
time: 88.6 us; the launch traced here: 88.4 us
  Pallas kernels  87.7 us (99%)
    pallas_call x1, Pallas kernels, gather(): pl.pallas_call(gather_kernel, out_shape=(jax.ShapeDtypeStruct(tshape, BF1...  28.4 us
    pallas_call x1, Pallas kernels, finish(): pl.pallas_call(finish_kernel, out_shape=(jax.ShapeDtypeStruct((2048, 128)...  22.8 us
    pallas_call x1, Pallas kernels, reduce_gram(): pl.pallas_call(reduce_kernel, out_shape=jax.ShapeDtypeStruct((16, 8, 128)...  20.4 us
    pallas_call x1, Pallas kernels, entries(): pl.pallas_call(entries_kernel, out_shape=(jax.ShapeDtypeStruct((2048, 128...  16.2 us

profile of v1, /device:TPU:1, one launch (start us, length us, event | category | flops | bytes accessed | tf_op | source)
XLA Modules:
  0.0 88.4 jit_solution(14406583614363801459)
XLA Ops:
  0.6 28.4 %gather.1 = (bf16[2,2,2,8,4,16,128]{6,5,4,3,2,1,0:T(8,128)(2,1)}, f32[2,2,2,8,4,1,128]{6,5,4,3,2,1,0:T(1,128)}) custom-call(bf16[16,128]{1,0:T(8,128)(2,1)} %bitcast.23, f32[1,16]{1,0:T(1,128)} %cd_in.1), custom_call_target="tpu_custom_call" | custom-call | tf_op jit(solution)/shard_map/gather/pallas_call | solution.py:182
  29.0 16.2 %entries.1 = (f32[2048,128]{1,0:T(8,128)}, f32[128,128]{1,0:T(8,128)}) custom-call(s32[4,64]{1,0:T(4,128)} %bitcast.19, s32[4,64]{1,0:T(4,128)} %bitcast.21, s32[4,64]{1,0:T(4,128)} %bitcast.26, s32[4]{0:T(128)} %bitcast.24, s32[4,64]{1,0:T(4,128)} %bitcast.20, s32[4,64]{1,0:T(4,128)} %bitcast.22, s32[1,4]{1,0:T(1,128)} %bitcast.25, ...), custom_call_target="tpu_custom_call" | custom-call | tf_op jit(solution)/shard_map/entries/pallas_call | solution.py:65
  45.2 20.4 %reduce.1 = f32[16,8,128]{2,1,0:T(8,128)} custom-call(f32[16,8,128]{2,1,0:T(8,128)} %bitcast.17), custom_call_target="tpu_custom_call" | custom-call | tf_op jit(solution)/shard_map/reduce/pallas_call | solution.py:244
  65.6 22.8 %finish.1 = (f32[2048,128]{1,0:T(8,128)}, f32[128,128]{1,0:T(8,128)}) custom-call(f32[128,128]{1,0:T(8,128)} %bitcast.15, f32[2048,128]{1,0:T(8,128)} %get-tuple-element.11.s_ref), custom_call_target="tpu_custom_call" | custom-call | tf_op jit(solution)/shard_map/finish/pallas_call | solution.py:112
